TPU v7x, 256 devices: a whole 4x4x8 slice. The times are simulated.
256 devices in a mesh: occ: 16 (over x_hi, y, core), ao: 16 (over x_lo, z).
Axes of the slice: x: 4 (x_hi: 2, x_lo: 2; x = x_hi * 2 + x_lo), y: 4, z: 8, core: 2. Of those that a mesh axis runs over, the one named last changes fastest.
Arguments:
- coef: bfloat16 [8192, 16], P('ao', 'occ'), may hold values from -0.25 to 0.25
- half_ints: bfloat16 [16, 1024, 8192], P('occ', None, 'ao'), may hold values from -0.5 to 0.5
- metric_inv: bfloat16 [64, 128, 128], replicated, may hold values from -1 to 2, as said below
- dom_blocks: int32 [16, 8], P('occ'), may hold values from 0 to 63, as said below
- dom_len: int32 [16], P('occ'), may hold values from 2 to 8
Outputs:
- exchange_k: float32 [8192, 8192], P('ao', 'occ')
- fit_density: float32 [8192], replicated
Inputs may be any that keep to these rules, and one draw needn't show every extreme that they name: `dom_blocks`: each row holds 8 different block numbers. `metric_inv`: full rank blocks.
All inputs are finite; a program needn't handle non-finite values.
Results may differ from a plain program's by a relative error of at most 0.0055.
Values may be sent and summed in bfloat16 or wider, within the bound.
A program may use at most 128 MiB of HBM per device.

v0:
```python
import jax
import jax.numpy as jnp
from jax import lax
from jax.sharding import PartitionSpec as P


def sent_to_all(x, axis):
    copies = jnp.broadcast_to(x, (lax.axis_size(axis), *x.shape))
    return lax.all_to_all(copies, axis, split_axis=0, concat_axis=0, tiled=True)


def over_copies(x, axis):
    everything = sent_to_all(x, axis)
    return jnp.sum(everything, axis=0)


def on_device(coef, half_ints, metric_inv, dom_blocks, dom_len):
    lmo_count, domain, ao_rows = half_ints.shape
    block = metric_inv.shape[1]
    slots = domain // block
    fit_blocks = metric_inv.shape[0]
    metric_rows = metric_inv[dom_blocks]
    raw_ints = half_ints.reshape(lmo_count, slots, block, ao_rows)
    fitted = jnp.einsum(
        "isab,isbm->isam", metric_rows, raw_ints, preferred_element_type=jnp.float32
    )
    live_slots = jnp.arange(slots, dtype=jnp.int32)[None, :] < dom_len[:, None]
    fitted = jnp.where(live_slots[:, :, None, None], fitted, 0.0)
    fitted = fitted.reshape(lmo_count, domain, ao_rows).astype(jnp.bfloat16)
    pair_part = jnp.einsum("ipm,mi->ip", fitted, coef, preferred_element_type=jnp.float32)
    one_hot = (
        dom_blocks[:, :, None] == jnp.arange(fit_blocks, dtype=jnp.int32)[None, None, :]
    ).astype(jnp.float32)
    pair_sum = over_copies(pair_part, "ao")
    local_density = jnp.einsum("isf,isr->fr", one_hot, pair_sum.reshape(lmo_count, slots, block))
    density = over_copies(local_density, "occ")
    density = density.reshape(fit_blocks * block)
    partial_value = jnp.einsum(
        "ipm,ipn->mn",
        fitted,
        lax.all_gather(fitted, "ao", axis=2, tiled=True),
        preferred_element_type=jnp.float32,
    )
    exchange_k = lax.psum_scatter(partial_value, "occ", scatter_dimension=1, tiled=True)
    return (exchange_k, density)


def solution(mesh):
    in_specs = (P("ao", "occ"), P("occ", None, "ao"), P(), P("occ", None), P("occ"))
    out_specs = (P("ao", "occ"), P())
    return jax.shard_map(
        on_device, mesh=mesh, in_specs=in_specs, out_specs=out_specs, check_vma=False
    )
```

profile of v0, /device:TPU:20, one launch (start us, length us, event | category | flops | bytes accessed | tf_op | source)
XLA Modules:
  0.0 372.1 jit_solution(9049975364195060182)
XLA Ops:
  7.2 0.0 copy-start
  7.2 0.0 all-gather.2.cloned.1.call-start
  8.0 0.7 fusion.7
  8.7 0.1 copy-done
  8.8 0.6 gather_fusion
  9.4 2.6 select_convert_fusion
  12.0 0.0 all-gather.2.cloned.1.call-update
  12.0 0.0 reduce-scatter.2.cloned.1.call-start
  12.1 187.8 %all-gather.2.cloned.1.call-done = bf16[1,1024,8192]{2,1,0:T(8,128)(2,1)} async-done(((bf16[1,1024,512]{2,1,0:T(8,128)(2,1)}), bf16[1,1024,8192]{2,1,0:T(8,128)(2,1)}) %all-gather.2.cloned.1.call-update) | async-done | bytes 16777232 | tf_op jit(solution)/shard_map/all_gather | solution.py:41
  199.9 16.0 %fusion = f32[512,8192]{1,0:T(8,128)} fusion(bf16[1024,512]{1,0:T(8,128)(2,1)} %bitcast.25, bf16[1,1024,8192]{2,1,0:T(8,128)(2,1)} %all-gather.2.cloned.1.call-done), kind=kOutput, calls=%fused_computation.1 | convolution fusion | flops 8589934592 | bytes 34603008 | tf_op jit(solution)/shard_map/ipm,ipn->mn/dot_general | solution.py:38
  215.8 0.0 copy-start.1
  215.8 0.0 copy-start.2
  215.8 0.0 reduce-scatter.2.cloned.1.call-update
  215.9 1.2 copy-done.1
  217.1 0.0 copy-done.2
  217.1 0.4 fusion.8
  217.4 0.1 broadcast_in_dim.29
  217.5 12.8 %all_to_all.10 = f32[16,1,1024]{2,1,0:T(1,128)S(1)} all-to-all(f32[16,1,1024]{2,1,0:T(1,128)S(1)} %broadcast_in_dim.29), channel_id=1, replica_groups=mesh['occ'=16,'ao'=16] {'ao'}, dimensions={0} | all-to-all | bytes 131072 | tf_op jit(solution)/shard_map/all_to_all | solution.py:9
  230.3 0.1 reduce_sum.18
  230.3 0.0 copy-done.3
  230.3 0.3 fusion.2
  230.7 15.0 %all_to_all.11 = f32[16,64,128]{2,1,0:T(8,128)S(1)} all-to-all(f32[16,64,128]{2,1,0:T(8,128)S(1)} %broadcast_in_dim.30), channel_id=1, replica_groups=mesh['occ'=16,'ao'=16] {'occ'}, dimensions={0} | all-to-all | bytes 1048576 | tf_op jit(solution)/shard_map/all_to_all | solution.py:9
  245.6 0.6 reduce_sum.19
  246.3 119.0 %reduce-scatter.2.cloned.1.call-done = f32[512,512]{1,0:T(8,128)} async-done(((f32[512,8192]{1,0:T(8,128)}), f32[512,512]{1,0:T(8,128)}) %reduce-scatter.2.cloned.1.call-update) | async-done | bytes 1048592 | tf_op jit(solution)/shard_map/reduce_scatter | solution.py:44
  (4 shorter events, 0.1 us)
Async XLA Ops:
  7.2 1.6 copy-start
  7.2 192.7 %all-gather.2.cloned.1.call-start = ((), (), s32[]{:S(2)}) async-start(), calls=%async_computation.3 | async-start | bytes 17825792 | tf_op jit(solution)/shard_map/all_gather | solution.py:41
  12.0 353.2 %reduce-scatter.2.cloned.1.call-start = ((), (), s32[]{:S(2)}) async-start(), calls=%async_computation.4 | async-start | bytes 17825792 | tf_op jit(solution)/shard_map/reduce_scatter | solution.py:44
  215.8 1.2 copy-start.1
  215.8 1.2 copy-start.2
  215.8 14.5 %copy-start.3 = (s32[1,8]{1,0:T(1,128)S(1)}, s32[1,8]{1,0:T(1,128)}, u32[]{:S(2)}) copy-start(s32[1,8]{1,0:T(1,128)} %param.8) | copy-start | bytes 100
Sparse Core Ops, SparseCore 0:
  12.2 187.6 all-gather.1
  216.0 149.2 reduce-scatter.1
where the time goes:
time: 377 us; the launch traced here: 372 us
  waiting for transfers between devices  307 us (81%)
  blocking collectives  27.7 us (7%)
  matrix products  19.2 us (5%)
  between operations  14.9 us (4%)
    all_gather x1, waiting for transfers between devices, on_device(): lax.all_gather(fitted, 'ao', axis=2, tiled=True)  188 us
    reduce_scatter x1, waiting for transfers between devices, on_device(): lax.psum_scatter(partial_value, 'occ', scatter_dimension=1, tiled=True)  119 us
    all_to_all x2, blocking collectives, sent_to_all(): return lax.all_to_all(copies, axis, split_axis=0, concat_axis=0, tiled=True)  27.7 us
    dot_general x1, matrix products, on_device(): jnp.einsum('ipm,ipn->mn', fitted, lax.all_gather(fitted, 'ao', axis=2, ti...  16 us
  transfers between devices with their start and end apart: 2, of which 2 were waited for; matrix products, arithmetic and copies ran while one was open for 0% of the time, Pallas kernels for 0%

commit v1 on v0

v1 whole, which is shorter than its diff:
```python
import jax
import jax.numpy as jnp
from jax import lax
from jax.experimental import pallas as pl
from jax.experimental.pallas import tpu as pltpu
from jax.sharding import PartitionSpec as P

MESH = pl.DeviceIdType.MESH
F32, BF16 = jnp.float32, jnp.bfloat16
RING = 8
CHUNKS = 4
CLASSES = (
    (0, 0, 0, False),
    (0, 1, 0, True),
    (-1, 1, 0, True),
    (1, 1, 1, False),
    (0, 1, 1, True),
    (-1, 1, 1, True),
    (-1, 2, 0, True),
    (-2, 1, 1, True),
    (-2, 2, 0, False),
    (-2, 2, 1, False),
)
EARLY = 6
NT = (((1,), (1,)), ((), ()))


def slot_of(offset, other):
    return offset + 4 if other else offset + 2


def wait_for(ref, sem):
    pltpu.make_async_copy(ref, ref, sem).wait()


def kernel(
    blocks_ref, len_ref, coef_ref, ints_ref, metric_ref,
    out_ref, dens_ref,
    held, give, core_in, local, summed, first_in, last_in, final, owned, pair_in, term_in,
    own_sem, pass_sem, chunk_sem, core_send, core_recv, sum_send, sum_recv,
    end_send, end_recv, pair_send, pair_recv, term_send, term_recv,
):
    occ, ao = lax.axis_index("occ"), lax.axis_index("ao")
    col, z = ao // RING, lax.rem(ao, RING)
    core, spot = lax.rem(occ, 2), occ // 2
    n_spots = RING
    width = held.shape[1]
    block = metric_ref.shape[1]
    slots = held.shape[2] // block
    rows = width // CHUNKS
    half = width // 2
    strip = half // n_spots

    def ao_at(c, dz):
        return c * RING + lax.rem(z + dz + RING, RING)

    up, down, across = ao_at(col, 1), ao_at(col, -1), ao_at(1 - col, 0)

    def chunk(slot, k):
        return held.at[slot, pl.ds(k * rows, rows), :]

    def send_chunk(src_slot, dst_slot, k, send_sem, to):
        pltpu.make_async_remote_copy(
            src_ref=chunk(src_slot, k), dst_ref=chunk(dst_slot, k), send_sem=send_sem,
            recv_sem=chunk_sem.at[dst_slot, k], device_id={"occ": occ, "ao": to}, device_id_type=MESH,
        ).start()

    def wait_chunk(slot, k):
        wait_for(chunk(slot, k), chunk_sem.at[slot, k])

    for k in range(CHUNKS):
        for s in range(slots):
            value = lax.dot_general(
                metric_ref[blocks_ref[0, s]], ints_ref[pl.ds(s * block, block), pl.ds(k * rows, rows)],
                (((1,), (0,)), ((), ())), preferred_element_type=F32,
            )
            live = jnp.full(value.shape, len_ref[0], jnp.int32) > s
            value = jnp.where(live, value, 0.0)
            held[2, pl.ds(k * rows, rows), pl.ds(s * block, block)] = value.T.astype(BF16)
        send_chunk(2, 1, k, own_sem.at[0], up)
        send_chunk(2, 3, k, own_sem.at[1], down)

    pair = lax.dot_general(
        coef_ref[...], held[2], (((1,), (0,)), ((), ())), preferred_element_type=F32
    )
    for s in range(slots):
        pair_in[ao, pl.ds(s, 1), :] = pair[0:1, s * block : (s + 1) * block]
    n_ao = pair_in.shape[0]
    for k in range(1, n_ao):
        pltpu.make_async_remote_copy(
            src_ref=pair_in.at[ao], dst_ref=pair_in.at[ao], send_sem=pair_send, recv_sem=pair_recv,
            device_id={"occ": occ, "ao": lax.rem(ao + k, n_ao)}, device_id_type=MESH,
        ).start()

    for k in range(CHUNKS):
        wait_chunk(1, k)
        send_chunk(1, 0, k, pass_sem.at[0], up)
        wait_chunk(3, k)
        send_chunk(3, 4, k, pass_sem.at[1], down)
        send_chunk(3, 5, k, pass_sem.at[2], across)

    wait_for(pair_in.at[pl.ds(0, n_ao - 1)], pair_recv)
    term = pair_in[0]
    for k in range(1, n_ao):
        term = term + pair_in[k]
    term_in[occ, pl.ds(0, slots), :] = term
    for s in range(slots):
        term_in[occ, pl.ds(slots + s, 1), :] = jnp.full((1, block), blocks_ref[0, s], jnp.int32).astype(F32)
    n_occ = term_in.shape[0]
    for k in range(1, n_occ):
        pltpu.make_async_remote_copy(
            src_ref=term_in.at[occ], dst_ref=term_in.at[occ], send_sem=term_send, recv_sem=term_recv,
            device_id={"occ": lax.rem(occ + k, n_occ), "ao": ao}, device_id_type=MESH,
        ).start()

    def product(c, which):
        i, t, other, _ = CLASSES[c]
        lhs = held[slot_of(i, 0), pl.ds(pl.multiple_of(which * half, half), half), :]
        return lax.dot_general(lhs, held[slot_of(t, other)], NT, preferred_element_type=F32)

    def for_other_core(c, g):
        give[c] = product(c, 1 - core).astype(BF16)
        pltpu.make_async_remote_copy(
            src_ref=give.at[c], dst_ref=core_in.at[c], send_sem=core_send.at[g], recv_sem=core_recv.at[g],
            device_id={"occ": occ + 1 - 2 * core, "ao": ao}, device_id_type=MESH,
        ).start()

    def sum_cores(lo, hi, g, arrived):
        n = hi - lo
        wait_for(core_in.at[pl.ds(lo, n)], core_recv.at[g])
        for c in range(lo, hi):
            summed[c] = (local[c] + core_in[c].astype(F32)).astype(BF16)
        for k in range(1, n_spots):
            peer = lax.rem(spot + k, n_spots)
            pltpu.make_async_remote_copy(
                src_ref=summed.at[pl.ds(lo, n), pl.ds(pl.multiple_of(peer * strip, strip), strip), :],
                dst_ref=arrived.at[k - 1], send_sem=sum_send.at[g], recv_sem=sum_recv.at[g],
                device_id={"occ": peer * 2 + core, "ao": ao}, device_id_type=MESH,
            ).start()

    place = pl.ds(pl.multiple_of((core * n_spots + spot) * strip, strip), strip)

    def deliveries(lo, hi):
        n = sum(1 + CLASSES[c][3] for c in range(lo))
        for c in range(lo, hi):
            i, t, other, both = CLASSES[c]
            first = ao_at(col, i)
            second = ao_at(1 - col if other else col, t)
            for occ_to, ao_to in ((second, first), (first, second))[: 1 + both]:
                yield n, c, occ_to, ao_to
                n += 1

    def deliver(lo, hi, g, arrived):
        n = hi - lo
        wait_for(arrived, sum_recv.at[g])
        for c in range(lo, hi):
            value = summed[c, pl.ds(pl.multiple_of(spot * strip, strip), strip), :].astype(F32)
            for k in range(n_spots - 1):
                value = value + arrived[k, c - lo].astype(F32)
            final[c] = value.astype(BF16)
        for m, c, occ_to, ao_to in deliveries(lo, hi):
            mine = jnp.logical_and(occ_to == occ, ao_to == ao)

            @pl.when(mine)
            def _():
                pltpu.make_async_copy(final.at[c], owned.at[place], end_recv).start()

            @pl.when(jnp.logical_not(mine))
            def _():
                pltpu.make_async_remote_copy(
                    src_ref=final.at[c], dst_ref=owned.at[place], send_sem=end_send.at[m], recv_sem=end_recv,
                    device_id={"occ": occ_to, "ao": ao_to}, device_id_type=MESH,
                ).start()

    n_classes = len(CLASSES)
    for c in range(3):
        for_other_core(c, 0)
    for k in range(CHUNKS):
        wait_chunk(5, k)
    for c in range(3, EARLY):
        for_other_core(c, 0)
    for c in range(EARLY):
        local[c] = product(c, core)
    sum_cores(0, EARLY, 0, first_in)

    for k in range(CHUNKS):
        wait_chunk(4, k)
        send_chunk(4, 6, k, pass_sem.at[3], across)
    for k in range(CHUNKS):
        wait_chunk(0, k)
    for c in range(EARLY, n_classes - 1):
        for_other_core(c, 1)
    for c in range(EARLY, n_classes - 1):
        local[c] = product(c, core)
    deliver(0, EARLY, 0, first_in)
    for k in range(CHUNKS):
        wait_chunk(6, k)
    for_other_core(n_classes - 1, 1)
    local[n_classes - 1] = product(n_classes - 1, core)
    sum_cores(EARLY, n_classes, 1, last_in)

    wait_for(term_in.at[pl.ds(0, n_occ - 1)], term_recv)
    terms = jnp.concatenate([term_in[i, 0:slots, :] for i in range(n_occ)], axis=0)
    numbers = jnp.concatenate([term_in[i, slots : 2 * slots, :] for i in range(n_occ)], axis=0)
    here = numbers == lax.broadcasted_iota(jnp.int32, numbers.shape, 1).astype(F32)
    full = lax.dot_general(
        here.astype(F32).T, terms, (((1,), (0,)), ((), ())),
        precision=lax.Precision.HIGHEST, preferred_element_type=F32,
    )
    dens_ref[...] = full[0 : dens_ref.shape[0]]

    deliver(EARLY, n_classes, 1, last_in)
    wait_for(owned, end_recv)
    turned = lax.rem(lax.rem(occ, RING) - z + RING, RING) > RING // 2

    @pl.when(turned)
    def _():
        out_ref[...] = owned[...].astype(F32).T

    @pl.when(jnp.logical_not(turned))
    def _():
        out_ref[...] = owned[...].astype(F32)

    wait_for(held.at[2], own_sem.at[0])
    wait_for(held.at[2], own_sem.at[1])
    for n in range(4):
        wait_for(held.at[0], pass_sem.at[n])
    wait_for(give.at[pl.ds(0, EARLY)], core_send.at[0])
    wait_for(give.at[pl.ds(EARLY, n_classes - EARLY)], core_send.at[1])
    wait_for(first_in, sum_send.at[0])
    wait_for(last_in, sum_send.at[1])
    wait_for(pair_in.at[pl.ds(0, n_ao - 1)], pair_send)
    wait_for(term_in.at[pl.ds(0, n_occ - 1)], term_send)
    for m, c, occ_to, ao_to in deliveries(0, n_classes):
        @pl.when(jnp.logical_not(jnp.logical_and(occ_to == occ, ao_to == ao)))
        def _():
            wait_for(final.at[c], end_send.at[m])


def on_device(coef, half_ints, metric_inv, dom_blocks, dom_len):
    _, domain, width = half_ints.shape
    fit_blocks, block, _ = metric_inv.shape
    slots = domain // block
    n = len(CLASSES)
    half, strip = width // 2, width // 2 // RING
    smem = pl.BlockSpec(memory_space=pltpu.SMEM)
    vmem = pl.BlockSpec(memory_space=pltpu.VMEM)
    dma = pltpu.SemaphoreType.DMA
    exchange, density = pl.pallas_call(
        kernel,
        out_shape=(
            jax.ShapeDtypeStruct((width, width), F32),
            jax.ShapeDtypeStruct((fit_blocks, block), F32),
        ),
        in_specs=[smem, smem, vmem, vmem, vmem],
        out_specs=(vmem, vmem),
        scratch_shapes=[
            pltpu.VMEM((7, width, domain), BF16),
            pltpu.VMEM((n, half, width), BF16),
            pltpu.VMEM((n, half, width), BF16),
            pltpu.VMEM((n, half, width), F32),
            pltpu.VMEM((n, half, width), BF16),
            pltpu.VMEM((RING - 1, EARLY, strip, width), BF16),
            pltpu.VMEM((RING - 1, n - EARLY, strip, width), BF16),
            pltpu.VMEM((n, strip, width), BF16),
            pltpu.VMEM((width, width), BF16),
            pltpu.VMEM((16, slots, block), F32),
            pltpu.VMEM((16, 2 * slots, block), F32),
            dma((2,)), dma((4,)), dma((7, CHUNKS)), dma((2,)), dma((2,)), dma((2,)), dma((2,)),
            dma((16,)), dma, dma, dma, dma, dma,
        ],
        compiler_params=pltpu.CompilerParams(vmem_limit_bytes=56 * 1024 * 1024, has_side_effects=True),
        cost_estimate=pl.CostEstimate(
            flops=n * 2 * width * width * domain, bytes_accessed=8 * 1024 * 1024, transcendentals=0
        ),
        name="exchange",
    )(dom_blocks, dom_len, coef.reshape(1, width), half_ints.reshape(domain, width), metric_inv)
    return exchange, density.reshape(fit_blocks * block)


def solution(mesh):
    in_specs = (P("ao", "occ"), P("occ", None, "ao"), P(), P("occ", None), P("occ"))
    out_specs = (P("ao", "occ"), P())
    return jax.shard_map(
        on_device, mesh=mesh, in_specs=in_specs, out_specs=out_specs, check_vma=False
    )
```

time: 377 us -> 134 us (0.36)
  the two profiles are of different devices: /device:TPU:20 before, /device:TPU:53 now
where the time goes in v1:
time: 134 us
  Pallas kernels  130 us (97%)
  local copies, waits for them, and re-layouts  2.89 us (2%)
    pallas_call x1, Pallas kernels, on_device(): pl.pallas_call(kernel, out_shape=(jax.ShapeDtypeStruct((width, width), F3...  130 us
    unnamed x4, local copies, waits for them, and re-layouts  2.89 us

profile of v1, /device:TPU:53, one launch (start us, length us, event | category | flops | bytes accessed | tf_op | source)
XLA Modules:
  0.0 134.2 jit_solution(7222921323684968115)
XLA Ops:
  1.3 130.0 %exchange.1 = (f32[512,512]{1,0:T(8,128)}, f32[64,128]{1,0:T(8,128)}) custom-call(s32[1,8]{1,0:T(1,128)} %blocks_ref.1, s32[1]{0:T(128)S(6)} %copy.9.len_ref, bf16[1,512]{1,0:T(2,128)(2,1)} %bitcast.5, bf16[1024,512]{1,0:T(8,128)(2,1)} %bitcast.4, bf16[64,128,128]{2,1,0:T(8,128)(2,1)} %metric_ref.1), custom_call_target="tpu_custom_call" | custom-call | flops 5368709120 | bytes 8388608 | tf_op jit(solution)/shard_map/exchange/pallas_call | solution.py:249
  131.3 0.0 copy-start
  131.3 2.3 %copy.10 = f32[512,512]{1,0:T(8,128)} copy(f32[512,512]{1,0:T(8,128)} %get-tuple-element.8) | data formatting | bytes 2097152
  133.5 0.0 copy-done
  133.5 0.6 copy.11
Async XLA Ops:
  131.3 2.3 %copy-start = (f32[64,128]{1,0:T(8,128)S(1)}, f32[64,128]{1,0:T(8,128)}, u32[]{:S(2)}) copy-start(f32[64,128]{1,0:T(8,128)} %get-tuple-element.5) | copy-start | bytes 98308

commit v2 on v1

v2 whole, which is shorter than its diff:
```python
import jax
import jax.numpy as jnp
from jax import lax
from jax.experimental import pallas as pl
from jax.experimental.pallas import tpu as pltpu
from jax.sharding import PartitionSpec as P

MESH = pl.DeviceIdType.MESH
F32, BF16 = jnp.float32, jnp.bfloat16
RING = 8
Y = 4
CHUNKS = 4
CLASSES = (
    (0, 0, 0, False),
    (0, 1, 0, True),
    (-1, 1, 0, True),
    (1, 1, 1, False),
    (0, 1, 1, True),
    (-1, 1, 1, True),
    (-2, 1, 0, True),
    (-2, 1, 1, True),
    (-2, 2, 0, False),
    (-2, 2, 1, False),
)
GROUPS = ((0, 1), (1, 3), (3, 6), (6, 9), (9, 10))
NT = (((1,), (1,)), ((), ()))


def slot_of(offset, other):
    return offset + 4 if other else offset + 2


def wait_for(ref, sem):
    pltpu.make_async_copy(ref, ref, sem).wait()


def kernel(
    blocks_ref, len_ref, coef_ref, ints_hbm, metric_hbm,
    out_ref, dens_ref,
    ints, metric, held, give, core_in, local, summed, y_in, y_sum, x_in, final, owned, pair_in, term_in,
    load_sem, own_sem, pass_sem, chunk_sem, core_send, core_recv, y_send, y_recv, x_send, x_recv,
    end_send, end_recv, pair_send, pair_recv, term_send, term_recv,
):
    occ, ao = lax.axis_index("occ"), lax.axis_index("ao")
    n_occ, n_ao = term_in.shape[0], pair_in.shape[0]
    barrier = pltpu.get_barrier_semaphore()
    for k in range(1, n_occ):
        pl.semaphore_signal(
            barrier, inc=1, device_id={"occ": lax.rem(occ + k, n_occ), "ao": ao}, device_id_type=MESH
        )
    for k in range(1, n_ao):
        pl.semaphore_signal(
            barrier, inc=1, device_id={"occ": occ, "ao": lax.rem(ao + k, n_ao)}, device_id_type=MESH
        )
    loads = (
        pltpu.make_async_copy(metric_hbm, metric, load_sem.at[0]),
        pltpu.make_async_copy(ints_hbm, ints, load_sem.at[1]),
    )
    for load in loads:
        load.start()

    col, z = ao // RING, lax.rem(ao, RING)
    core = lax.rem(occ, 2)
    y, x = lax.rem(occ // 2, Y), occ // (2 * Y)
    width, domain = held.shape[1], held.shape[2]
    block = metric.shape[1]
    slots = domain // block
    rows = width // CHUNKS
    half = width // 2
    part = half // Y
    strip = part // 2

    def ao_at(c, dz):
        return c * RING + lax.rem(z + dz + RING, RING)

    up, down, across = ao_at(col, 1), ao_at(col, -1), ao_at(1 - col, 0)

    def send(src, dst, send_sem, recv_sem, occ_to, ao_to):
        pltpu.make_async_remote_copy(
            src_ref=src, dst_ref=dst, send_sem=send_sem, recv_sem=recv_sem,
            device_id={"occ": occ_to, "ao": ao_to}, device_id_type=MESH,
        ).start()

    def chunk(slot, k):
        return held.at[slot, pl.ds(k * rows, rows), :]

    def send_chunk(src_slot, dst_slot, k, send_sem, to):
        send(chunk(src_slot, k), chunk(dst_slot, k), send_sem, chunk_sem.at[dst_slot, k], occ, to)

    def wait_chunk(slot, k):
        wait_for(chunk(slot, k), chunk_sem.at[slot, k])

    for load in loads:
        load.wait()
    for k in range(CHUNKS):
        for s in range(slots):
            value = lax.dot_general(
                metric[blocks_ref[0, s]], ints[pl.ds(s * block, block), pl.ds(k * rows, rows)],
                (((1,), (0,)), ((), ())), preferred_element_type=F32,
            )
            live = jnp.full(value.shape, len_ref[0], jnp.int32) > s
            value = jnp.where(live, value, 0.0)
            held[2, pl.ds(k * rows, rows), pl.ds(s * block, block)] = value.T.astype(BF16)
        if k == 0:
            pl.semaphore_wait(barrier, n_occ + n_ao - 2)
        send_chunk(2, 1, k, own_sem.at[0], up)
        send_chunk(2, 3, k, own_sem.at[1], down)

    def product(c, which):
        i, t, other, _ = CLASSES[c]
        lhs = held[slot_of(i, 0), pl.ds(pl.multiple_of(which * half, half), half), :]
        return lax.dot_general(lhs, held[slot_of(t, other)], NT, preferred_element_type=F32)

    def multiply(g):
        for c in range(*GROUPS[g]):
            give[c] = product(c, 1 - core).astype(BF16)
            send(give.at[c], core_in.at[c], core_send.at[g], core_recv.at[g], occ + 1 - 2 * core, ao)
        for c in range(*GROUPS[g]):
            local[c] = product(c, core)

    def span(g):
        lo, hi = GROUPS[g]
        return pl.ds(lo, hi - lo)

    def sum_cores(g):
        wait_for(core_in.at[span(g)], core_recv.at[g])
        for c in range(*GROUPS[g]):
            summed[c] = (local[c] + core_in[c].astype(F32)).astype(BF16)
        for k in (1, 3, 2):
            to = lax.rem(y + k, Y)
            send(
                summed.at[span(g), pl.ds(pl.multiple_of(to * part, part), part), :], y_in.at[k - 1, span(g)],
                y_send.at[g], y_recv.at[g], x * (2 * Y) + to * 2 + core, ao,
            )

    def sum_y(g):
        wait_for(y_in.at[:, span(g)], y_recv.at[g])
        for c in range(*GROUPS[g]):
            value = summed[c, pl.ds(pl.multiple_of(y * part, part), part), :].astype(F32)
            for k in range(Y - 1):
                value = value + y_in[k, c].astype(F32)
            y_sum[c] = value.astype(BF16)
        send(
            y_sum.at[span(g), pl.ds(pl.multiple_of((1 - x) * strip, strip), strip), :], x_in.at[span(g)],
            x_send.at[g], x_recv.at[g], (1 - x) * (2 * Y) + y * 2 + core, ao,
        )

    place = pl.ds(pl.multiple_of((core * (2 * Y) + y * 2 + x) * strip, strip), strip)

    def deliveries(lo, hi):
        n = sum(1 + CLASSES[c][3] for c in range(lo))
        for c in range(lo, hi):
            i, t, other, both = CLASSES[c]
            first = ao_at(col, i)
            second = ao_at(1 - col if other else col, t)
            for occ_to, ao_to in ((second, first), (first, second))[: 1 + both]:
                yield n, c, occ_to, ao_to
                n += 1

    def deliver(g):
        wait_for(x_in.at[span(g)], x_recv.at[g])
        for c in range(*GROUPS[g]):
            value = y_sum[c, pl.ds(pl.multiple_of(x * strip, strip), strip), :].astype(F32)
            final[c] = (value + x_in[c].astype(F32)).astype(BF16)
        for m, c, occ_to, ao_to in deliveries(*GROUPS[g]):
            mine = jnp.logical_and(occ_to == occ, ao_to == ao)

            @pl.when(mine)
            def _():
                pltpu.make_async_copy(final.at[c], owned.at[place], end_recv).start()

            @pl.when(jnp.logical_not(mine))
            def _():
                send(final.at[c], owned.at[place], end_send.at[m], end_recv, occ_to, ao_to)

    def pass_on(k):
        wait_chunk(1, k)
        send_chunk(1, 0, k, pass_sem.at[0], up)
        wait_chunk(3, k)
        send_chunk(3, 4, k, pass_sem.at[1], down)
        send_chunk(3, 5, k, pass_sem.at[2], across)

    def pass_across(k):
        wait_chunk(4, k)
        send_chunk(4, 6, k, pass_sem.at[3], across)

    pair = lax.dot_general(
        coef_ref[...], held[2], (((1,), (0,)), ((), ())), preferred_element_type=F32
    )
    for s in range(slots):
        pair_in[ao, pl.ds(s, 1), :] = pair[0:1, s * block : (s + 1) * block]
    for k in range(1, n_ao):
        send(pair_in.at[ao], pair_in.at[ao], pair_send, pair_recv, occ, lax.rem(ao + k, n_ao))

    multiply(0)
    pass_on(0)
    sum_cores(0)
    pass_on(1)

    wait_for(pair_in.at[pl.ds(0, n_ao - 1)], pair_recv)
    term = pair_in[0]
    for k in range(1, n_ao):
        term = term + pair_in[k]
    term_in[occ, pl.ds(0, slots), :] = term
    for s in range(slots):
        term_in[occ, pl.ds(slots + s, 1), :] = jnp.full((1, block), blocks_ref[0, s], jnp.int32).astype(F32)
    for k in range(1, n_occ):
        send(term_in.at[occ], term_in.at[occ], term_send, term_recv, lax.rem(occ + k, n_occ), ao)

    pass_on(2)
    sum_y(0)
    pass_on(3)
    multiply(1)
    sum_cores(1)
    for k in range(CHUNKS):
        wait_chunk(5, k)
    multiply(2)
    pass_across(0)
    sum_cores(2)
    deliver(0)
    pass_across(1)
    sum_y(1)
    pass_across(2)
    sum_y(2)
    pass_across(3)
    for k in range(CHUNKS):
        wait_chunk(0, k)
    multiply(3)
    sum_cores(3)
    deliver(1)
    for k in range(CHUNKS):
        wait_chunk(6, k)
    multiply(4)
    sum_cores(4)
    deliver(2)

    wait_for(term_in.at[pl.ds(0, n_occ - 1)], term_recv)
    terms = jnp.concatenate([term_in[i, 0:slots, :] for i in range(n_occ)], axis=0)
    numbers = jnp.concatenate([term_in[i, slots : 2 * slots, :] for i in range(n_occ)], axis=0)
    here = numbers == lax.broadcasted_iota(jnp.int32, numbers.shape, 1).astype(F32)
    full = lax.dot_general(
        here.astype(F32).T, terms, (((1,), (0,)), ((), ())),
        precision=lax.Precision.HIGHEST, preferred_element_type=F32,
    )
    dens_ref[...] = full[0 : dens_ref.shape[0]]

    sum_y(3)
    sum_y(4)
    deliver(3)
    deliver(4)
    wait_for(owned, end_recv)
    turned = lax.rem(lax.rem(occ, RING) - z + RING, RING) > RING // 2

    @pl.when(turned)
    def _():
        out_ref[...] = owned[...].astype(F32).T.astype(BF16)

    @pl.when(jnp.logical_not(turned))
    def _():
        out_ref[...] = owned[...]

    wait_for(held.at[2], own_sem.at[0])
    wait_for(held.at[2], own_sem.at[1])
    for n in range(4):
        wait_for(held.at[0], pass_sem.at[n])
    for g in range(len(GROUPS)):
        wait_for(give.at[span(g)], core_send.at[g])
        wait_for(y_in.at[:, span(g)], y_send.at[g])
        wait_for(x_in.at[span(g)], x_send.at[g])
    wait_for(pair_in.at[pl.ds(0, n_ao - 1)], pair_send)
    wait_for(term_in.at[pl.ds(0, n_occ - 1)], term_send)
    for m, c, occ_to, ao_to in deliveries(0, len(CLASSES)):
        @pl.when(jnp.logical_not(jnp.logical_and(occ_to == occ, ao_to == ao)))
        def _():
            wait_for(final.at[c], end_send.at[m])


def on_device(coef, half_ints, metric_inv, dom_blocks, dom_len):
    _, domain, width = half_ints.shape
    fit_blocks, block, _ = metric_inv.shape
    slots = domain // block
    n = len(CLASSES)
    half = width // 2
    part = half // Y
    smem = pl.BlockSpec(memory_space=pltpu.SMEM)
    vmem = pl.BlockSpec(memory_space=pltpu.VMEM)
    hbm = pl.BlockSpec(memory_space=pl.ANY)
    dma = pltpu.SemaphoreType.DMA
    per_group = dma((len(GROUPS),))
    exchange, density = pl.pallas_call(
        kernel,
        out_shape=(
            jax.ShapeDtypeStruct((width, width), BF16),
            jax.ShapeDtypeStruct((fit_blocks, block), F32),
        ),
        in_specs=[smem, smem, vmem, hbm, hbm],
        out_specs=(vmem, vmem),
        scratch_shapes=[
            pltpu.VMEM((domain, width), BF16),
            pltpu.VMEM((fit_blocks, block, block), BF16),
            pltpu.VMEM((7, width, domain), BF16),
            pltpu.VMEM((n, half, width), BF16),
            pltpu.VMEM((n, half, width), BF16),
            pltpu.VMEM((n, half, width), F32),
            pltpu.VMEM((n, half, width), BF16),
            pltpu.VMEM((Y - 1, n, part, width), BF16),
            pltpu.VMEM((n, part, width), BF16),
            pltpu.VMEM((n, part // 2, width), BF16),
            pltpu.VMEM((n, part // 2, width), BF16),
            pltpu.VMEM((width, width), BF16),
            pltpu.VMEM((16, slots, block), F32),
            pltpu.VMEM((16, 2 * slots, block), F32),
            dma((2,)), dma((2,)), dma((4,)), dma((7, CHUNKS)),
            per_group, per_group, per_group, per_group, per_group, per_group,
            dma((16,)), dma, dma, dma, dma, dma,
        ],
        compiler_params=pltpu.CompilerParams(
            vmem_limit_bytes=56 * 1024 * 1024, has_side_effects=True, collective_id=0
        ),
        cost_estimate=pl.CostEstimate(
            flops=n * 2 * width * width * domain, bytes_accessed=8 * 1024 * 1024, transcendentals=0
        ),
        name="exchange",
    )(dom_blocks, dom_len, coef.reshape(1, width), half_ints.reshape(domain, width), metric_inv)
    return exchange.astype(F32), density.reshape(fit_blocks * block)


def solution(mesh):
    in_specs = (P("ao", "occ"), P("occ", None, "ao"), P(), P("occ", None), P("occ"))
    out_specs = (P("ao", "occ"), P())
    return jax.shard_map(
        on_device, mesh=mesh, in_specs=in_specs, out_specs=out_specs, check_vma=False
    )
```

time: 134 us -> 110 us (0.82)
  the two profiles are of different devices: /device:TPU:53 before, /device:TPU:20 now
where the time goes in v2:
time: 110 us; the launch traced here: 108 us
  Pallas kernels  103 us (94%)
  other arithmetic  2.15 us (2%)
  local copies, waits for them, and re-layouts  1.37 us (1%)
  between operations  1.29 us (1%)
    pallas_call x1, Pallas kernels, on_device(): pl.pallas_call(kernel, out_shape=(jax.ShapeDtypeStruct((width, width), BF...  103 us

profile of v2, /device:TPU:20, one launch (start us, length us, event | category | flops | bytes accessed | tf_op | source)
XLA Modules:
  0.0 107.7 jit_solution(9046895045929829994)
XLA Ops:
  1.3 102.9 %exchange.1 = (bf16[512,512]{1,0:T(8,128)(2,1)}, f32[64,128]{1,0:T(8,128)}) custom-call(s32[1,8]{1,0:T(1,128)} %blocks_ref.1, s32[1]{0:T(128)S(6)} %copy.8.len_ref, bf16[1,512]{1,0:T(2,128)(2,1)} %bitcast.5, bf16[1024,512]{1,0:T(8,128)(2,1)} %bitcast.4, bf16[64,128,128]{2,1,0:T(8,128)(2,1)} %metric_hbm.1), custom_call_target="tpu_custom_call" | custom-call | flops 5368709120 | bytes 8388608 | tf_op jit(solution)/shard_map/exchange/pallas_call | solution.py:290
  104.2 2.1 %convert_element_type.3 = f32[512,512]{1,0:T(8,128)} convert(bf16[512,512]{1,0:T(8,128)(2,1)} %get-tuple-element.4) | non-fusion elementwise | flops 262144 | bytes 1572864 | tf_op jit(solution)/shard_map/convert_element_type | solution.py:325
  106.3 1.4 %copy.9 = f32[8192]{0:T(1024)} copy(f32[8192]{0:T(1024)} %bitcast.3) | data formatting | bytes 65536

commit v3 on v2

v3 whole, which is shorter than its diff:
```python
import jax
import jax.numpy as jnp
from jax import lax
from jax.experimental import pallas as pl
from jax.experimental.pallas import tpu as pltpu
from jax.sharding import PartitionSpec as P

MESH = pl.DeviceIdType.MESH
F32, BF16 = jnp.float32, jnp.bfloat16
RING = 8
Y = 4
CHUNKS = 8
PLAN = (
    ((0, 0, 0, False, 0, 2),),
    ((0, 1, 0, True, 0, 2), (-1, 1, 0, True, 0, 2)),
    ((1, 1, 1, False, 0, 2), (0, 1, 1, True, 0, 2), (-1, 1, 1, True, 0, 2)),
    ((-2, 1, 0, True, 0, 1), (-2, 1, 1, True, 0, 1)),
    ((-2, 1, 0, True, 1, 1), (-2, 1, 1, True, 1, 1), "opposite"),
    ("across",),
)
UNITS, SENDS = 19, 22
NT = (((1,), (1,)), ((), ()))


def wait_for(ref, sem):
    pltpu.make_async_copy(ref, ref, sem).wait()


def kernel(
    blocks_ref, len_ref, coef_ref, ints_hbm, metric_hbm,
    out_ref, dens_ref,
    ints, metric, held, give, core_in, local, summed, y_in, y_sum, x_in, final, owned, pair_in, term_in,
    load_sem, own_sem, pass_sem, chunk_sem, core_send, core_recv, y_send, y_recv, x_send, x_recv,
    end_send, end_recv, pair_send, pair_recv, term_send, term_recv,
):
    occ, ao = lax.axis_index("occ"), lax.axis_index("ao")
    n_occ, n_ao = term_in.shape[0], pair_in.shape[0]
    barrier = pltpu.get_barrier_semaphore()
    for k in range(1, n_occ):
        pl.semaphore_signal(
            barrier, inc=1, device_id={"occ": lax.rem(occ + k, n_occ), "ao": ao}, device_id_type=MESH
        )
    for k in range(1, n_ao):
        pl.semaphore_signal(
            barrier, inc=1, device_id={"occ": occ, "ao": lax.rem(ao + k, n_ao)}, device_id_type=MESH
        )
    loads = (
        pltpu.make_async_copy(metric_hbm, metric, load_sem.at[0]),
        pltpu.make_async_copy(ints_hbm, ints, load_sem.at[1]),
    )
    for load in loads:
        load.start()

    col, z = ao // RING, lax.rem(ao, RING)
    core = lax.rem(occ, 2)
    y, x = lax.rem(occ // 2, Y), occ // (2 * Y)
    width, domain = held.shape[1], held.shape[2]
    block = metric.shape[1]
    slots = domain // block
    rows = width // CHUNKS
    half = width // 2
    quarter = half // 2
    part = quarter // Y
    strip = part // 2
    depth = domain // 2

    def ao_at(c, dz):
        return c * RING + lax.rem(z + dz + RING, RING)

    up, down, across = ao_at(col, 1), ao_at(col, -1), ao_at(1 - col, 0)

    def send(src, dst, send_sem, recv_sem, occ_to, ao_to):
        pltpu.make_async_remote_copy(
            src_ref=src, dst_ref=dst, send_sem=send_sem, recv_sem=recv_sem,
            device_id={"occ": occ_to, "ao": ao_to}, device_id_type=MESH,
        ).start()

    def chunk(slot, k):
        return held.at[slot, pl.ds(k * rows, rows), :]

    def send_chunk(src_slot, dst_slot, k, send_sem, to):
        send(chunk(src_slot, k), chunk(dst_slot, k), send_sem, chunk_sem.at[dst_slot, k], occ, to)

    def wait_chunk(slot, k):
        wait_for(chunk(slot, k), chunk_sem.at[slot, k])

    for load in loads:
        load.wait()
    for k in range(0, width, block):
        for s in range(slots):
            value = lax.dot_general(
                metric[blocks_ref[0, s]], ints[pl.ds(s * block, block), pl.ds(k, block)],
                (((1,), (0,)), ((), ())), preferred_element_type=F32,
            )
            live = jnp.full(value.shape, len_ref[0], jnp.int32) > s
            value = jnp.where(live, value, 0.0)
            held[2, pl.ds(k, block), pl.ds(s * block, block)] = value.T.astype(BF16)
        if k == 0:
            pl.semaphore_wait(barrier, n_occ + n_ao - 2)
        for m in range(k // rows, (k + block) // rows):
            send_chunk(2, 1, m, own_sem.at[0], up)
            send_chunk(2, 3, m, own_sem.at[1], down)

    groups, unit = [], 0
    upper = z // (RING // 2)
    for plan in PLAN:
        group = []
        for entry in plan:
            whole = (0, domain)
            if entry == "opposite":
                group.append((
                    unit, 1, 4 - 4 * upper, upper, 4 * upper, whole,
                    ao_at(col, 2 - 4 * upper), ao_at(col, 4 * upper - 2), True, 0,
                ))
            elif entry == "across":
                group.append((
                    unit, 2, 6 * col, 0, 6 - 2 * col, (pl.multiple_of(col * depth, depth), depth),
                    ao_at(0, -2), ao_at(1, 2), True, col,
                ))
            else:
                i, t, other, both, first, n = entry
                group.append((
                    unit, n, i + 2, first, t + 4 if other else t + 2, whole,
                    ao_at(col, i), ao_at(1 - col if other else col, t), both, 0,
                ))
            unit += group[-1][1]
        groups.append(group)

    def span(g):
        lo = groups[g][0][0]
        return pl.ds(lo, groups[g][-1][0] + groups[g][-1][1] - lo)

    def units(g):
        at = span(g)
        return range(at.start, at.start + at.size)

    def multiply(g):
        for u, n, left, first, right, (lo, size), *_ in groups[g]:
            for m in range(n):
                at = pl.ds(pl.multiple_of((first + m) * half, half), half)
                local[u + m] = lax.dot_general(
                    held[left, at, pl.ds(lo, size)], held[right, :, pl.ds(lo, size)], NT,
                    preferred_element_type=F32,
                )
                other = local[u + m, pl.ds(pl.multiple_of((1 - core) * quarter, quarter), quarter), :]
                give[u + m] = other.astype(BF16)
            send(
                give.at[pl.ds(u, n)], core_in.at[pl.ds(u, n)], core_send.at[g], core_recv.at[g],
                occ + 1 - 2 * core, ao,
            )

    def sum_cores(g):
        wait_for(core_in.at[span(g)], core_recv.at[g])
        for u in units(g):
            mine = local[u, pl.ds(pl.multiple_of(core * quarter, quarter), quarter), :]
            summed[u] = (mine + core_in[u].astype(F32)).astype(BF16)
        for k in (1, 3, 2):
            to = lax.rem(y + k, Y)
            send(
                summed.at[span(g), pl.ds(pl.multiple_of(to * part, part), part), :], y_in.at[k - 1, span(g)],
                y_send.at[g], y_recv.at[g], x * (2 * Y) + to * 2 + core, ao,
            )

    def sum_y(g):
        wait_for(y_in.at[:, span(g)], y_recv.at[g])
        for u in units(g):
            value = summed[u, pl.ds(pl.multiple_of(y * part, part), part), :].astype(F32)
            for k in range(Y - 1):
                value = value + y_in[k, u].astype(F32)
            y_sum[u] = value.astype(BF16)
        send(
            y_sum.at[span(g), pl.ds(pl.multiple_of((1 - x) * strip, strip), strip), :], x_in.at[span(g)],
            x_send.at[g], x_recv.at[g], (1 - x) * (2 * Y) + y * 2 + core, ao,
        )

    place = pl.ds(pl.multiple_of(core * quarter + (y * 2 + x) * strip, strip), strip)
    trips, number = [], 0
    for group in groups:
        trip = []
        for u, n, _, first, _, _, row_block, column_block, both, part_of in group:
            for occ_to, ao_to in ((column_block, row_block), (row_block, column_block))[: 1 + both]:
                mine = jnp.logical_and(occ_to == occ, ao_to == ao)
                trip.append((number, u, n, first, part_of, occ_to, ao_to, mine))
                number += 1
        trips.append(trip)

    def deliver(g):
        wait_for(x_in.at[span(g)], x_recv.at[g])
        for u in units(g):
            value = y_sum[u, pl.ds(pl.multiple_of(x * strip, strip), strip), :].astype(F32)
            final[u] = (value + x_in[u].astype(F32)).astype(BF16)
        for m, u, n, first, part_of, occ_to, ao_to, mine in trips[g]:
            src, dst = final.at[pl.ds(u, n)], owned.at[part_of, pl.ds(first, n), place, :]

            @pl.when(mine)
            def _():
                pltpu.make_async_copy(src, dst, end_recv.at[part_of]).start()

            @pl.when(jnp.logical_not(mine))
            def _():
                send(src, dst, end_send.at[m], end_recv.at[part_of], occ_to, ao_to)

    def pass_on(k):
        wait_chunk(1, k)
        send_chunk(1, 0, k, pass_sem.at[0], up)
        wait_chunk(3, k)
        send_chunk(3, 4, k, pass_sem.at[1], down)
        send_chunk(3, 5, k, pass_sem.at[2], across)

    def half_chunk(slot, k, which):
        return held.at[slot, pl.ds(k * rows, rows), pl.ds(pl.multiple_of(which * depth, depth), depth)]

    def pass_across(k):
        wait_chunk(0, k)
        wait_chunk(4, k)
        send(
            half_chunk(4 * col, k, 1 - col), half_chunk(6, k, 1 - col), pass_sem.at[3], chunk_sem.at[6, k],
            occ, across,
        )

    pass_on(0)
    multiply(0)
    pass_on(1)
    pair = lax.dot_general(
        coef_ref[...], held[2], (((1,), (0,)), ((), ())), preferred_element_type=F32
    )
    for s in range(slots):
        pair_in[ao, pl.ds(s, 1), :] = pair[0:1, s * block : (s + 1) * block]
    for k in range(1, n_ao):
        send(pair_in.at[ao], pair_in.at[ao], pair_send, pair_recv, occ, lax.rem(ao + k, n_ao))
    pass_on(2)
    sum_cores(0)
    pass_on(3)
    pass_on(4)
    pass_on(5)
    pass_on(6)
    pass_on(7)
    multiply(1)
    pass_across(0)
    sum_cores(1)
    pass_across(1)
    for k in range(CHUNKS):
        wait_chunk(5, k)
    multiply(2)
    pass_across(2)
    sum_cores(2)
    pass_across(3)
    multiply(3)
    sum_cores(3)
    pass_across(4)
    sum_y(0)
    sum_y(1)
    pass_across(5)
    pass_across(6)
    wait_for(pair_in.at[pl.ds(0, n_ao - 1)], pair_recv)
    term = pair_in[0]
    for k in range(1, n_ao):
        term = term + pair_in[k]
    term_in[occ, pl.ds(0, slots), :] = term
    for s in range(slots):
        term_in[occ, pl.ds(slots + s, 1), :] = jnp.full((1, block), blocks_ref[0, s], jnp.int32).astype(F32)
    for k in range(1, n_occ):
        send(term_in.at[occ], term_in.at[occ], term_send, term_recv, lax.rem(occ + k, n_occ), ao)

    pass_across(7)
    multiply(4)
    sum_y(2)
    sum_y(3)
    sum_cores(4)
    deliver(0)
    deliver(1)
    for k in range(CHUNKS):
        wait_for(half_chunk(6, k, col), chunk_sem.at[6, k])
    multiply(5)
    sum_cores(5)
    deliver(2)
    wait_for(term_in.at[pl.ds(0, n_occ - 1)], term_recv)
    terms = jnp.concatenate([term_in[i, 0:slots, :] for i in range(n_occ)], axis=0)
    numbers = jnp.concatenate([term_in[i, slots : 2 * slots, :] for i in range(n_occ)], axis=0)
    here = numbers == lax.broadcasted_iota(jnp.int32, numbers.shape, 1).astype(F32)
    full = lax.dot_general(
        here.astype(F32).T, terms, (((1,), (0,)), ((), ())),
        precision=lax.Precision.HIGHEST, preferred_element_type=F32,
    )
    dens_ref[...] = full[0 : dens_ref.shape[0]]

    deliver(3)
    sum_y(4)
    sum_y(5)
    deliver(4)
    deliver(5)
    difference = lax.rem(lax.rem(occ, RING) - z + RING, RING)
    far, same = difference == RING // 2, occ // RING == col
    below = jnp.logical_or(z < 2, z >= 2 + RING // 2)
    turned = jnp.logical_or(
        difference > RING // 2,
        jnp.logical_and(far, jnp.where(same, below.astype(jnp.int32), col) > 0),
    )
    wait_for(owned.at[0], end_recv.at[0])

    @pl.when(jnp.logical_and(far, jnp.logical_not(same)))
    def _():
        wait_for(owned.at[1], end_recv.at[1])
        owned[0] = (owned[0].astype(F32) + owned[1].astype(F32)).astype(BF16)

    @pl.when(turned)
    def _():
        out_ref[...] = owned[0].reshape(width, width).astype(F32).T.astype(BF16)

    @pl.when(jnp.logical_not(turned))
    def _():
        out_ref[...] = owned[0].reshape(width, width)

    wait_for(held.at[2], own_sem.at[0])
    wait_for(held.at[2], own_sem.at[1])
    for n in range(3):
        wait_for(held.at[0], pass_sem.at[n])
    wait_for(held.at[6, :, pl.ds(0, depth)], pass_sem.at[3])
    for g in range(len(PLAN)):
        wait_for(give.at[span(g)], core_send.at[g])
        wait_for(y_in.at[:, span(g)], y_send.at[g])
        wait_for(x_in.at[span(g)], x_send.at[g])
    wait_for(pair_in.at[pl.ds(0, n_ao - 1)], pair_send)
    wait_for(term_in.at[pl.ds(0, n_occ - 1)], term_send)
    for trip in trips:
        for m, u, n, *_, mine in trip:
            @pl.when(jnp.logical_not(mine))
            def _():
                wait_for(final.at[pl.ds(u, n)], end_send.at[m])


def on_device(coef, half_ints, metric_inv, dom_blocks, dom_len):
    _, domain, width = half_ints.shape
    fit_blocks, block, _ = metric_inv.shape
    slots = domain // block
    half = width // 2
    quarter = half // 2
    part = quarter // Y
    smem = pl.BlockSpec(memory_space=pltpu.SMEM)
    vmem = pl.BlockSpec(memory_space=pltpu.VMEM)
    hbm = pl.BlockSpec(memory_space=pl.ANY)
    dma = pltpu.SemaphoreType.DMA
    per_group = dma((len(PLAN),))
    exchange, density = pl.pallas_call(
        kernel,
        out_shape=(
            jax.ShapeDtypeStruct((width, width), BF16),
            jax.ShapeDtypeStruct((fit_blocks, block), F32),
        ),
        in_specs=[smem, smem, vmem, hbm, hbm],
        out_specs=(vmem, vmem),
        scratch_shapes=[
            pltpu.VMEM((domain, width), BF16),
            pltpu.VMEM((fit_blocks, block, block), BF16),
            pltpu.VMEM((7, width, domain), BF16),
            pltpu.VMEM((UNITS, quarter, width), BF16),
            pltpu.VMEM((UNITS, quarter, width), BF16),
            pltpu.VMEM((UNITS, half, width), F32),
            pltpu.VMEM((UNITS, quarter, width), BF16),
            pltpu.VMEM((Y - 1, UNITS, part, width), BF16),
            pltpu.VMEM((UNITS, part, width), BF16),
            pltpu.VMEM((UNITS, part // 2, width), BF16),
            pltpu.VMEM((UNITS, part // 2, width), BF16),
            pltpu.VMEM((2, 2, half, width), BF16),
            pltpu.VMEM((16, slots, block), F32),
            pltpu.VMEM((16, 2 * slots, block), F32),
            dma((2,)), dma((2,)), dma((4,)), dma((7, CHUNKS)),
            per_group, per_group, per_group, per_group, per_group, per_group,
            dma((SENDS,)), dma((2,)), dma, dma, dma, dma,
        ],
        compiler_params=pltpu.CompilerParams(
            vmem_limit_bytes=56 * 1024 * 1024, has_side_effects=True, collective_id=0
        ),
        cost_estimate=pl.CostEstimate(
            flops=UNITS * width * width * domain, bytes_accessed=8 * 1024 * 1024, transcendentals=0
        ),
        name="exchange",
    )(dom_blocks, dom_len, coef.reshape(1, width), half_ints.reshape(domain, width), metric_inv)
    return exchange.astype(F32), density.reshape(fit_blocks * block)


def solution(mesh):
    in_specs = (P("ao", "occ"), P("occ", None, "ao"), P(), P("occ", None), P("occ"))
    out_specs = (P("ao", "occ"), P())
    return jax.shard_map(
        on_device, mesh=mesh, in_specs=in_specs, out_specs=out_specs, check_vma=False
    )
```

time: 110 us -> 92.6 us (0.84); the launches traced: 108 us -> 92.4 us
  Pallas kernels: 103 us -> 87.6 us
    pallas_call x1, Pallas kernels: 103 us -> 87.6 us  [on_device(): pl.pallas_call(kernel, out_shape=(jax.ShapeDtypeStruct((width, width), BF...]
where the time goes in v3:
time: 92.6 us; the launch traced here: 92.4 us
  Pallas kernels  87.6 us (95%)
  other arithmetic  2.15 us (2%)
  local copies, waits for them, and re-layouts  1.37 us (1%)
  between operations  1.29 us (1%)
    pallas_call x1, Pallas kernels, on_device(): pl.pallas_call(kernel, out_shape=(jax.ShapeDtypeStruct((width, width), BF...  87.6 us
    convert_element_type x1, other arithmetic, on_device(): return (exchange.astype(F32), density.reshape(fit_blocks * block))  2.15 us

profile of v3, /device:TPU:20, one launch (start us, length us, event | category | flops | bytes accessed | tf_op | source)
XLA Modules:
  0.0 92.4 jit_solution(14934524325988907099)
XLA Ops:
  1.3 87.6 %exchange.1 = (bf16[512,512]{1,0:T(8,128)(2,1)}, f32[64,128]{1,0:T(8,128)}) custom-call(s32[1,8]{1,0:T(1,128)} %blocks_ref.1, s32[1]{0:T(128)S(6)} %copy.8.len_ref, bf16[1,512]{1,0:T(2,128)(2,1)} %bitcast.5, bf16[1024,512]{1,0:T(8,128)(2,1)} %bitcast.4, bf16[64,128,128]{2,1,0:T(8,128)(2,1)} %metric_hbm.1), custom_call_target="tpu_custom_call" | custom-call | flops 5100273664 | bytes 8388608 | tf_op jit(solution)/shard_map/exchange/pallas_call | solution.py:344
  88.8 2.1 %convert_element_type.3 = f32[512,512]{1,0:T(8,128)} convert(bf16[512,512]{1,0:T(8,128)(2,1)} %get-tuple-element.4) | non-fusion elementwise | flops 262144 | bytes 1572864 | tf_op jit(solution)/shard_map/convert_element_type | solution.py:379
  91.0 1.4 %copy.9 = f32[8192]{0:T(1024)} copy(f32[8192]{0:T(1024)} %bitcast.3) | data formatting | bytes 65536

commit v4 on v3

--- a/solution.py
+++ b/solution.py
@@ -15,10 +15,10 @@
     ((0, 1, 0, True, 0, 2), (-1, 1, 0, True, 0, 2)),
     ((1, 1, 1, False, 0, 2), (0, 1, 1, True, 0, 2), (-1, 1, 1, True, 0, 2)),
     ((-2, 1, 0, True, 0, 1), (-2, 1, 1, True, 0, 1)),
-    ((-2, 1, 0, True, 1, 1), (-2, 1, 1, True, 1, 1), "opposite"),
+    ((-2, 1, 0, True, 1, 1), "opposite", (-2, 1, 1, True, 1, 1)),
     ("across",),
 )
-UNITS, SENDS = 19, 22
+UNITS, SENDS, RUNS = 19, 22, 8
 NT = (((1,), (1,)), ((), ()))
 
 
@@ -61,7 +61,6 @@
     half = width // 2
     quarter = half // 2
     part = quarter // Y
-    strip = part // 2
     depth = domain // 2
 
     def ao_at(c, dz):
@@ -110,18 +109,18 @@
             if entry == "opposite":
                 group.append((
                     unit, 1, 4 - 4 * upper, upper, 4 * upper, whole,
-                    ao_at(col, 2 - 4 * upper), ao_at(col, 4 * upper - 2), True, 0,
+                    ao_at(col, 2 - 4 * upper), ao_at(col, 4 * upper - 2), True, 0, 0,
                 ))
             elif entry == "across":
                 group.append((
                     unit, 2, 6 * col, 0, 6 - 2 * col, (pl.multiple_of(col * depth, depth), depth),
-                    ao_at(0, -2), ao_at(1, 2), True, col,
+                    ao_at(0, -2), ao_at(1, 2), True, col, 1,
                 ))
             else:
                 i, t, other, both, first, n = entry
                 group.append((
                     unit, n, i + 2, first, t + 4 if other else t + 2, whole,
-                    ao_at(col, i), ao_at(1 - col if other else col, t), both, 0,
+                    ao_at(col, i), ao_at(1 - col if other else col, t), both, 0, other,
                 ))
             unit += group[-1][1]
         groups.append(group)
@@ -168,37 +167,50 @@
             for k in range(Y - 1):
                 value = value + y_in[k, u].astype(F32)
             y_sum[u] = value.astype(BF16)
-        send(
-            y_sum.at[span(g), pl.ds(pl.multiple_of((1 - x) * strip, strip), strip), :], x_in.at[span(g)],
-            x_send.at[g], x_recv.at[g], (1 - x) * (2 * Y) + y * 2 + core, ao,
-        )
-
-    place = pl.ds(pl.multiple_of(core * quarter + (y * 2 + x) * strip, strip), strip)
-    trips, number = [], 0
+        for r, at, keeper, _ in runs[g]:
+            @pl.when(x != keeper)
+            def _():
+                send(
+                    y_sum.at[at], x_in.at[at], x_send.at[r], x_recv.at[r], (1 - x) * (2 * Y) + y * 2 + core, ao,
+                )
+
+    place = pl.ds(pl.multiple_of(core * quarter + y * part, part), part)
+    runs, run, number = [], 0, 0
     for group in groups:
-        trip = []
-        for u, n, _, first, _, _, row_block, column_block, both, part_of in group:
-            for occ_to, ao_to in ((column_block, row_block), (row_block, column_block))[: 1 + both]:
-                mine = jnp.logical_and(occ_to == occ, ao_to == ao)
-                trip.append((number, u, n, first, part_of, occ_to, ao_to, mine))
-                number += 1
-        trips.append(trip)
+        of_group = []
+        for other in (0, 1):
+            trip, first_unit, n_units = [], None, 0
+            for u, n, _, first, _, _, row_block, column_block, both, part_of, kind in group:
+                if kind != other:
+                    continue
+                first_unit = u if first_unit is None else first_unit
+                n_units += n
+                for occ_to, ao_to in ((column_block, row_block), (row_block, column_block))[: 1 + both]:
+                    mine = jnp.logical_and(occ_to == occ, ao_to == ao)
+                    trip.append((number, u, n, first, part_of, occ_to, ao_to, mine))
+                    number += 1
+            if trip:
+                of_group.append((run, pl.ds(first_unit, n_units), 1 - col if other else col, trip))
+                run += 1
+        runs.append(of_group)
 
     def deliver(g):
-        wait_for(x_in.at[span(g)], x_recv.at[g])
-        for u in units(g):
-            value = y_sum[u, pl.ds(pl.multiple_of(x * strip, strip), strip), :].astype(F32)
-            final[u] = (value + x_in[u].astype(F32)).astype(BF16)
-        for m, u, n, first, part_of, occ_to, ao_to, mine in trips[g]:
-            src, dst = final.at[pl.ds(u, n)], owned.at[part_of, pl.ds(first, n), place, :]
-
-            @pl.when(mine)
+        for r, at, keeper, trip in runs[g]:
+            @pl.when(x == keeper)
             def _():
-                pltpu.make_async_copy(src, dst, end_recv.at[part_of]).start()
-
-            @pl.when(jnp.logical_not(mine))
-            def _():
-                send(src, dst, end_send.at[m], end_recv.at[part_of], occ_to, ao_to)
+                wait_for(x_in.at[at], x_recv.at[r])
+                for u in range(at.start, at.start + at.size):
+                    final[u] = (y_sum[u].astype(F32) + x_in[u].astype(F32)).astype(BF16)
+                for m, u, n, first, part_of, occ_to, ao_to, mine in trip:
+                    src, dst = final.at[pl.ds(u, n)], owned.at[part_of, pl.ds(first, n), place, :]
+
+                    @pl.when(mine)
+                    def _():
+                        pltpu.make_async_copy(src, dst, end_recv.at[part_of]).start()
+
+                    @pl.when(jnp.logical_not(mine))
+                    def _():
+                        send(src, dst, end_send.at[m], end_recv.at[part_of], occ_to, ao_to)
 
     def pass_on(k):
         wait_chunk(1, k)
@@ -238,6 +250,7 @@
     multiply(1)
     pass_across(0)
     sum_cores(1)
+    sum_y(0)
     pass_across(1)
     for k in range(CHUNKS):
         wait_chunk(5, k)
@@ -248,10 +261,12 @@
     multiply(3)
     sum_cores(3)
     pass_across(4)
-    sum_y(0)
     sum_y(1)
+    deliver(0)
     pass_across(5)
+    sum_y(2)
     pass_across(6)
+    deliver(1)
     wait_for(pair_in.at[pl.ds(0, n_ao - 1)], pair_recv)
     term = pair_in[0]
     for k in range(1, n_ao):
@@ -264,16 +279,14 @@
 
     pass_across(7)
     multiply(4)
-    sum_y(2)
     sum_y(3)
     sum_cores(4)
-    deliver(0)
-    deliver(1)
+    deliver(2)
     for k in range(CHUNKS):
         wait_for(half_chunk(6, k, col), chunk_sem.at[6, k])
     multiply(5)
     sum_cores(5)
-    deliver(2)
+    deliver(3)
     wait_for(term_in.at[pl.ds(0, n_occ - 1)], term_recv)
     terms = jnp.concatenate([term_in[i, 0:slots, :] for i in range(n_occ)], axis=0)
     numbers = jnp.concatenate([term_in[i, slots : 2 * slots, :] for i in range(n_occ)], axis=0)
@@ -284,7 +297,6 @@
     )
     dens_ref[...] = full[0 : dens_ref.shape[0]]
 
-    deliver(3)
     sum_y(4)
     sum_y(5)
     deliver(4)
@@ -319,14 +331,23 @@
     for g in range(len(PLAN)):
         wait_for(give.at[span(g)], core_send.at[g])
         wait_for(y_in.at[:, span(g)], y_send.at[g])
-        wait_for(x_in.at[span(g)], x_send.at[g])
     wait_for(pair_in.at[pl.ds(0, n_ao - 1)], pair_send)
     wait_for(term_in.at[pl.ds(0, n_occ - 1)], term_send)
-    for trip in trips:
-        for m, u, n, *_, mine in trip:
-            @pl.when(jnp.logical_not(mine))
+    for of_group in runs:
+        for r, at, keeper, trip in of_group:
+            @pl.when(x != keeper)
             def _():
-                wait_for(final.at[pl.ds(u, n)], end_send.at[m])
+                wait_for(x_in.at[at], x_send.at[r])
+
+            for m, u, n, *_, mine in trip:
+                @pl.when(jnp.logical_and(x == keeper, jnp.logical_not(mine)))
+                def _():
+                    wait_for(final.at[pl.ds(u, n)], end_send.at[m])
+
+
+def widen(block_ref, dens_ref, out_ref, dens_out_ref):
+    out_ref[...] = block_ref[...].astype(F32)
+    dens_out_ref[...] = dens_ref[...]
 
 
 def on_device(coef, half_ints, metric_inv, dom_blocks, dom_len):
@@ -359,13 +380,13 @@
             pltpu.VMEM((UNITS, quarter, width), BF16),
             pltpu.VMEM((Y - 1, UNITS, part, width), BF16),
             pltpu.VMEM((UNITS, part, width), BF16),
-            pltpu.VMEM((UNITS, part // 2, width), BF16),
-            pltpu.VMEM((UNITS, part // 2, width), BF16),
+            pltpu.VMEM((UNITS, part, width), BF16),
+            pltpu.VMEM((UNITS, part, width), BF16),
             pltpu.VMEM((2, 2, half, width), BF16),
             pltpu.VMEM((16, slots, block), F32),
             pltpu.VMEM((16, 2 * slots, block), F32),
             dma((2,)), dma((2,)), dma((4,)), dma((7, CHUNKS)),
-            per_group, per_group, per_group, per_group, per_group, per_group,
+            per_group, per_group, per_group, per_group, dma((RUNS,)), dma((RUNS,)),
             dma((SENDS,)), dma((2,)), dma, dma, dma, dma,
         ],
         compiler_params=pltpu.CompilerParams(
@@ -376,7 +397,17 @@
         ),
         name="exchange",
     )(dom_blocks, dom_len, coef.reshape(1, width), half_ints.reshape(domain, width), metric_inv)
-    return exchange.astype(F32), density.reshape(fit_blocks * block)
+    exchange, density = pl.pallas_call(
+        widen,
+        out_shape=(
+            jax.ShapeDtypeStruct((width, width), F32),
+            jax.ShapeDtypeStruct((fit_blocks, block), F32),
+        ),
+        in_specs=[vmem, vmem],
+        out_specs=(vmem, vmem),
+        name="widen",
+    )(exchange, density)
+    return exchange, density.reshape(fit_blocks * block)
 
 
 def solution(mesh):

time: 92.6 us -> 90.5 us (0.977)
  other arithmetic: 2.15 us -> 0 us
  local copies, waits for them, and re-layouts: 1.37 us -> 0 us
  Pallas kernels: 87.6 us -> 88.6 us
    convert_element_type x1 -> x0, other arithmetic: 2.15 us -> none  [on_device(): return (exchange.astype(F32), density.reshape(fit_blocks * block))]
    pallas_call x0 -> x1, Pallas kernels: none -> 2.09 us  [on_device(): pl.pallas_call(widen, out_shape=(jax.ShapeDtypeStruct((width, width), F32...]
    unnamed x1 -> x0, local copies, waits for them, and re-layouts: 1.37 us -> none
    pallas_call x1, Pallas kernels: 87.6 us -> 86.5 us  [on_device(): pl.pallas_call(kernel, out_shape=(jax.ShapeDtypeStruct((width, width), BF...]
where the time goes in v4:
time: 90.5 us; the launch traced here: 89.9 us
  Pallas kernels  88.6 us (98%)
  between operations  1.29 us (1%)
    pallas_call x1, Pallas kernels, on_device(): pl.pallas_call(kernel, out_shape=(jax.ShapeDtypeStruct((width, width), BF...  86.5 us
    pallas_call x1, Pallas kernels, on_device(): pl.pallas_call(widen, out_shape=(jax.ShapeDtypeStruct((width, width), F32...  2.09 us

profile of v4, /device:TPU:20, one launch (start us, length us, event | category | flops | bytes accessed | tf_op | source)
XLA Modules:
  0.0 89.9 jit_solution(3194772482144855484)
XLA Ops:
  1.3 86.5 %exchange.1 = (bf16[512,512]{1,0:T(8,128)(2,1)}, f32[64,128]{1,0:T(8,128)}) custom-call(s32[1,8]{1,0:T(1,128)} %blocks_ref.1, s32[1]{0:T(128)S(6)} %copy.7.len_ref, bf16[1,512]{1,0:T(2,128)(2,1)} %bitcast.5, bf16[1024,512]{1,0:T(8,128)(2,1)} %bitcast.3, bf16[64,128,128]{2,1,0:T(8,128)(2,1)} %metric_hbm.1), custom_call_target="tpu_custom_call" | custom-call | flops 5100273664 | bytes 8388608 | tf_op jit(solution)/shard_map/exchange/pallas_call | solution.py:365
  87.8 2.1 %widen.1 = (f32[512,512]{1,0:T(8,128)}, f32[64,128]{1,0:T(8,128)}) custom-call(bf16[512,512]{1,0:T(8,128)(2,1)} %get-tuple-element.6.block_ref, f32[64,128]{1,0:T(8,128)} %get-tuple-element.7.dens_ref), custom_call_target="tpu_custom_call" | custom-call | tf_op jit(solution)/shard_map/widen/pallas_call | solution.py:400

commit v5 on v4

--- a/solution.py
+++ b/solution.py
@@ -153,7 +153,7 @@
         for u in units(g):
             mine = local[u, pl.ds(pl.multiple_of(core * quarter, quarter), quarter), :]
             summed[u] = (mine + core_in[u].astype(F32)).astype(BF16)
-        for k in (1, 3, 2):
+        for k in (2, 1, 3):
             to = lax.rem(y + k, Y)
             send(
                 summed.at[span(g), pl.ds(pl.multiple_of(to * part, part), part), :], y_in.at[k - 1, span(g)],

time: 90.5 us -> 91 us (level)
  Pallas kernels: 88.6 us -> 89.6 us
    pallas_call x1, Pallas kernels: 86.5 us -> 87.5 us  [on_device(): pl.pallas_call(kernel, out_shape=(jax.ShapeDtypeStruct((width, width), BF...]
where the time goes in v5:
time: 91 us; the launch traced here: 90.8 us
  Pallas kernels  89.6 us (98%)
  between operations  1.29 us (1%)
    pallas_call x1, Pallas kernels, on_device(): pl.pallas_call(kernel, out_shape=(jax.ShapeDtypeStruct((width, width), BF...  87.5 us
    pallas_call x1, Pallas kernels, on_device(): pl.pallas_call(widen, out_shape=(jax.ShapeDtypeStruct((width, width), F32...  2.09 us

profile of v5, /device:TPU:20, one launch (start us, length us, event | category | flops | bytes accessed | tf_op | source)
XLA Modules:
  0.0 90.8 jit_solution(9342354763877951461)
XLA Ops:
  1.3 87.5 %exchange.1 = (bf16[512,512]{1,0:T(8,128)(2,1)}, f32[64,128]{1,0:T(8,128)}) custom-call(s32[1,8]{1,0:T(1,128)} %blocks_ref.1, s32[1]{0:T(128)S(6)} %copy.7.len_ref, bf16[1,512]{1,0:T(2,128)(2,1)} %bitcast.5, bf16[1024,512]{1,0:T(8,128)(2,1)} %bitcast.3, bf16[64,128,128]{2,1,0:T(8,128)(2,1)} %metric_hbm.1), custom_call_target="tpu_custom_call" | custom-call | flops 5100273664 | bytes 8388608 | tf_op jit(solution)/shard_map/exchange/pallas_call | solution.py:365
  88.7 2.1 %widen.1 = (f32[512,512]{1,0:T(8,128)}, f32[64,128]{1,0:T(8,128)}) custom-call(bf16[512,512]{1,0:T(8,128)(2,1)} %get-tuple-element.6.block_ref, f32[64,128]{1,0:T(8,128)} %get-tuple-element.7.dens_ref), custom_call_target="tpu_custom_call" | custom-call | tf_op jit(solution)/shard_map/widen/pallas_call | solution.py:400
